TPU v7x, 32 devices: a whole 2x2x4 slice. The times are simulated.
32 devices in a mesh: dp: 8 (over z, x), mp: 4 (over y, core).
Axes of the slice: x: 2, y: 2, z: 4, core: 2. Of those that a mesh axis runs over, the one named last changes fastest.
Arguments:
- tokens_in: bfloat16 [8, 1024, 2048], P('dp'), may hold values from -6 to 6
- cotangent: bfloat16 [8, 1024, 2048], P('dp'), may hold values from -6 to 6
- select_mask: int32 [8, 1024], P('dp'), may hold values 0 or 1
- doc_ids: int32 [8, 1024], P('dp'), may hold values from 0 to 3, never falling along the last dimension, each value on 1 to 512 neighbouring positions
- norm_gains: float32 [2, 2048], replicated, may hold values from 0.5 to 1.5
- weight_blocks: float32 [2688, 128, 128], P(('dp', 'mp'))
- ema_blocks: float32 [2688, 128, 128], P(('dp', 'mp')), may hold values from -1.5 to 1.5
- left_stats: float32 [2688, 128, 128], P(('dp', 'mp')), as said below
- right_stats: float32 [2688, 128, 128], P(('dp', 'mp')), as said below
- left_roots: float32 [2688, 128, 128], P(('dp', 'mp')), as said below
- right_roots: float32 [2688, 128, 128], P(('dp', 'mp')), as said below
Outputs:
- block_out: bfloat16 [8, 1024, 2048], P('dp')
- input_grad: float32 [8, 1024, 2048], P('dp')
- block_grads: float32 [2688, 128, 128], P(('dp', 'mp'))
- new_weights: float32 [2688, 128, 128], P(('dp', 'mp'))
- new_ema: float32 [2688, 128, 128], P(('dp', 'mp'))
- new_left: float32 [2688, 128, 128], P(('dp', 'mp'))
- new_right: float32 [2688, 128, 128], P(('dp', 'mp'))
- gain_grads: float32 [2, 2048], P(None, 'dp')
- new_gains: float32 [2, 2048], P(None, 'dp')
Inputs may be any that keep to these rules, and one draw needn't show every extreme that they name: `doc_ids`: within each sequence the ids never fall; every one of the 4 documents has 1 to 512 positions. `left_stats`: each block is symmetric. `right_stats`: each block is symmetric. `left_roots`: each block is symmetric. `right_roots`: each block is symmetric.
All inputs are finite; a program needn't handle non-finite values. No bound on the sum of `select_mask` on one device may be relied on, other than what follows from the above.
Results may differ from a plain program's by a relative error of at most 0.015.
The roundings to bfloat16 on the way count: a program that leaves them out, or rounds other values in their place, can miss the bound.
Values may be sent and summed in bfloat16 or wider, within the bound.
No kernel may reach another device: no remote copies, remote signals or barrier semaphores. Data moves between devices by JAX's collectives and lax.ppermute only.
A program may use at most 320 MiB of HBM per device.

v0:
```python
import jax
import jax.numpy as jnp
from jax import lax
from jax.sharding import PartitionSpec as P

HEADS = 32
KV_HEADS = 4
HD = 64
FF = 5632
highest = lax.Precision.HIGHEST
weight_rate = 1.0
gain_rate = 0.2
average_decay = 0.9


def doc_positions(doc_ids):
    length = doc_ids.shape[-1]
    offsets = jnp.arange(length, dtype=jnp.int32)
    starts = jnp.concatenate(
        [jnp.ones(doc_ids.shape[:-1] + (1,), jnp.bool_), doc_ids[..., 1:] != doc_ids[..., :-1]],
        axis=-1,
    )
    first_index = lax.cummax(jnp.where(starts, offsets, 0), axis=doc_ids.ndim - 1)
    return offsets - first_index


def rope_tables(positions, head_size):
    half_size = head_size // 2
    exponent = jnp.arange(half_size, dtype=jnp.float32) * (2.0 / head_size)
    inverse = jnp.power(jnp.float32(10000.0), -exponent)
    angles = positions.astype(jnp.float32)[..., None] * inverse
    return (jnp.cos(angles), jnp.sin(angles))


def rotate(values, cosine_table, sine_table):
    half_size = values.shape[-1] // 2
    first_half = values[..., :half_size]
    second_half = values[..., half_size:]
    return jnp.concatenate(
        [
            first_half * cosine_table - second_half * sine_table,
            second_half * cosine_table + first_half * sine_table,
        ],
        axis=-1,
    )


def rotate_back(grads, cosine_table, sine_table):
    half_size = grads.shape[-1] // 2
    first_half = grads[..., :half_size]
    second_half = grads[..., half_size:]
    return jnp.concatenate(
        [
            first_half * cosine_table + second_half * sine_table,
            second_half * cosine_table - first_half * sine_table,
        ],
        axis=-1,
    )


def normalize(values, gain):
    inverse_rms = lax.rsqrt(jnp.mean(values * values, axis=-1, keepdims=True) + 1e-05)
    unit = values * inverse_rms
    return (unit * gain, unit, inverse_rms)


def normalize_back(grad_out, unit, inverse_rms, gain):
    scaled = grad_out * gain
    return inverse_rms * (scaled - unit * jnp.mean(scaled * unit, axis=-1, keepdims=True))


def project(inputs, weights):
    row_count = inputs.shape[0]
    shaped = inputs.reshape(row_count, weights.shape[0], weights.shape[-1])
    return jnp.einsum("tri,rcij->tcj", shaped, weights, preferred_element_type=jnp.float32).reshape(
        row_count, -1
    )


def project_back(grads, weights):
    row_count = grads.shape[0]
    shaped = grads.reshape(row_count, weights.shape[1], weights.shape[-1])
    return jnp.einsum("tcj,rcij->tri", shaped, weights, preferred_element_type=jnp.float32).reshape(
        row_count, -1
    )


def weight_grad(inputs, grads, block_size):
    row_count = inputs.shape[0]
    left_shaped = inputs.reshape(row_count, -1, block_size)
    right_shaped = grads.reshape(row_count, -1, block_size)
    return jnp.einsum(
        "tri,tcj->rcij", left_shaped, right_shaped, preferred_element_type=jnp.float32
    )


def split_weights(gathered, row_blocks, attn_blocks, in_blocks, out_attn_blocks):
    block_size = gathered.shape[-1]
    in_count = row_blocks * in_blocks
    w_input = gathered[:in_count].reshape(row_blocks, in_blocks, block_size, block_size)
    w_output = gathered[in_count:].reshape(-1, row_blocks, block_size, block_size)
    return (
        w_input[:, :attn_blocks],
        w_input[:, attn_blocks:],
        w_output[:out_attn_blocks],
        w_output[out_attn_blocks:],
    )


def block_scores(query_part, keys, doc_ids, offset, scale):
    row_count = query_part.shape[0]
    query_index = offset + jnp.arange(row_count)
    key_index = jnp.arange(keys.shape[0])
    allowed = (key_index[None, :] <= query_index[:, None]) & (
        doc_ids[None, :] == doc_ids[offset : offset + row_count][:, None]
    )
    scores = (
        jnp.einsum("qgjd,kgd->gjqk", query_part, keys, preferred_element_type=jnp.float32) * scale
    )
    return jnp.where(allowed, scores, -1e30)


def attend_forward(queries, keys, values, doc_ids, query_block):
    length = queries.shape[0]
    scale = float(queries.shape[-1]) ** (-0.5)
    outputs = []
    totals = []
    for offset in range(0, length, query_block):
        scores = block_scores(queries[offset : offset + query_block], keys, doc_ids, offset, scale)
        maximum = jnp.max(scores, axis=-1, keepdims=True)
        expo_values = jnp.exp(scores - maximum)
        denominator = jnp.sum(expo_values, axis=-1, keepdims=True)
        probs = (expo_values / denominator).astype(jnp.bfloat16)
        outputs.append(
            jnp.einsum("gjqk,kgd->qgjd", probs, values, preferred_element_type=jnp.float32)
        )
        totals.append(maximum + jnp.log(denominator))
    return (jnp.concatenate(outputs, axis=0), jnp.concatenate(totals, axis=2))


def attend_backward(queries, keys, values, doc_ids, log_totals, out_grads, query_block):
    length = queries.shape[0]
    scale = float(queries.shape[-1]) ** (-0.5)
    key_grads = jnp.zeros(keys.shape, jnp.float32)
    value_grads = jnp.zeros(values.shape, jnp.float32)
    query_grads = []
    for offset in range(0, length, query_block):
        query_part = queries[offset : offset + query_block]
        scores = block_scores(query_part, keys, doc_ids, offset, scale)
        probs = jnp.exp(scores - log_totals[:, :, offset : offset + query_block])
        grad_part = out_grads[offset : offset + query_block]
        value_grads = value_grads + jnp.einsum(
            "gjqk,qgjd->kgd",
            probs.astype(jnp.bfloat16),
            grad_part,
            preferred_element_type=jnp.float32,
        )
        prob_grads = jnp.einsum(
            "qgjd,kgd->gjqk", grad_part, values, preferred_element_type=jnp.float32
        )
        inner = jnp.sum(probs * prob_grads, axis=-1, keepdims=True)
        score_grads = (probs * (prob_grads - inner)).astype(jnp.bfloat16)
        query_grads.append(
            jnp.einsum("gjqk,kgd->qgjd", score_grads, keys, preferred_element_type=jnp.float32)
            * scale
        )
        key_grads = (
            key_grads
            + jnp.einsum(
                "gjqk,qgjd->kgd", score_grads, query_part, preferred_element_type=jnp.float32
            )
            * scale
        )
    return (jnp.concatenate(query_grads, axis=0), key_grads, value_grads)


def ring_order(count):
    return list(range(0, count, 2)) + list(range(1, count, 2))[::-1]


def sum_rows(values):
    return lax.psum_scatter(
        values.astype(jnp.bfloat16), "mp", scatter_dimension=0, tiled=True
    ).astype(jnp.float32)


def on_device(
    tokens_in,
    cotangent,
    select_mask,
    doc_ids,
    norm_gains,
    weight_blocks,
    ema_blocks,
    left_stats,
    right_stats,
    left_roots,
    right_roots,
):
    mp_count = lax.axis_size("mp")
    dp_count = lax.axis_size("dp")
    sequences, length, model_width = tokens_in.shape
    row_count = sequences * length
    block_size = weight_blocks.shape[-1]
    query_cols = HEADS * HD // mp_count
    key_cols = KV_HEADS * HD // mp_count
    hidden_cols = FF // mp_count
    kv_local = KV_HEADS // mp_count
    group_size = HEADS // KV_HEADS
    row_blocks = model_width // block_size
    attn_blocks = (query_cols + 2 * key_cols) // block_size
    in_blocks = attn_blocks + 2 * hidden_cols // block_size
    out_attn_blocks = query_cols // block_size
    query_block = min(512, length)
    share_rows = row_count // mp_count
    share_start = lax.axis_index("mp") * share_rows

    def row_share(values):
        return lax.dynamic_slice_in_dim(values, share_start, share_rows, 0)

    ring = ring_order(dp_count)
    places = [ring.index(rank) for rank in range(dp_count)]
    own = weight_blocks.shape[0]
    weights_low = weight_blocks.astype(jnp.bfloat16)
    in_ring = lax.all_gather(weights_low, "dp", axis=0, tiled=True, axis_index_groups=[ring])
    gathered = jnp.concatenate(
        [in_ring[place * own : (place + 1) * own] for place in places], axis=0
    )
    w_qkv, w_gateup, w_attn_out, w_down = split_weights(
        gathered, row_blocks, attn_blocks, in_blocks, out_attn_blocks
    )
    positions = doc_positions(doc_ids)
    cosine_table, sine_table = rope_tables(positions, HD)
    query_cos = cosine_table[:, :, None, None, :]
    query_sin = sine_table[:, :, None, None, :]
    key_cos = cosine_table[:, :, None, :]
    key_sin = sine_table[:, :, None, :]
    tokens = tokens_in.astype(jnp.float32).reshape(row_count, model_width)
    first_norm, first_unit, first_scale = normalize(tokens, norm_gains[0])
    first_in = first_norm.astype(jnp.bfloat16)
    qkv = project(first_in, w_qkv)
    queries_raw = qkv[:, :query_cols].reshape(sequences, length, kv_local, group_size, HD)
    keys_raw = qkv[:, query_cols : query_cols + key_cols].reshape(sequences, length, kv_local, HD)
    values_raw = qkv[:, query_cols + key_cols :].reshape(sequences, length, kv_local, HD)
    query_use = rotate(queries_raw, query_cos, query_sin).astype(jnp.bfloat16)
    key_use = rotate(keys_raw, key_cos, key_sin).astype(jnp.bfloat16)
    value_use = values_raw.astype(jnp.bfloat16)

    def forward_one(items):
        return attend_forward(items[0], items[1], items[2], items[3], query_block)

    mixed, log_totals = lax.map(forward_one, (query_use, key_use, value_use, doc_ids))
    mixed_use = mixed.reshape(row_count, query_cols).astype(jnp.bfloat16)
    attended_part = sum_rows(project(mixed_use, w_attn_out))
    middle = row_share(tokens) + attended_part
    second_norm, second_unit, second_scale = normalize(middle, norm_gains[1])
    second_in = lax.all_gather(second_norm.astype(jnp.bfloat16), "mp", axis=0, tiled=True)
    gateup = project(second_in, w_gateup)
    gate = gateup[:, :hidden_cols]
    up_part = gateup[:, hidden_cols:]
    sigmoid_gate = jax.nn.sigmoid(gate)
    hidden = (gate * sigmoid_gate * up_part).astype(jnp.bfloat16)
    feed_part = sum_rows(project(hidden, w_down))
    out_whole = lax.all_gather((middle + feed_part).astype(jnp.bfloat16), "mp", axis=0, tiled=True)
    block_out = out_whole.reshape(sequences, length, model_width)
    out_grad = cotangent.astype(jnp.float32).reshape(row_count, model_width) * select_mask.astype(
        jnp.float32
    ).reshape(row_count, 1)
    mlp_grad = out_grad.astype(jnp.bfloat16)
    grad_down = weight_grad(hidden, mlp_grad, block_size)
    hidden_grad = project_back(mlp_grad, w_down)
    gate_grad = hidden_grad * up_part * sigmoid_gate * (1.0 + gate * (1.0 - sigmoid_gate))
    up_grad = hidden_grad * gate * sigmoid_gate
    gateup_grad = jnp.concatenate([gate_grad, up_grad], axis=1).astype(jnp.bfloat16)
    grad_gateup = weight_grad(second_in, gateup_grad, block_size)
    second_grad = sum_rows(project_back(gateup_grad, w_gateup))
    middle_grad = row_share(out_grad) + normalize_back(
        second_grad, second_unit, second_scale, norm_gains[1]
    )
    second_gain = jnp.sum(second_grad * second_unit, axis=0)
    attn_grad = lax.all_gather(middle_grad.astype(jnp.bfloat16), "mp", axis=0, tiled=True)
    grad_attn_out = weight_grad(mixed_use, attn_grad, block_size)
    mixed_grad = (
        project_back(attn_grad, w_attn_out)
        .astype(jnp.bfloat16)
        .reshape(sequences, length, kv_local, group_size, HD)
    )

    def backward_one(items):
        return attend_backward(
            items[0], items[1], items[2], items[3], items[4], items[5], query_block
        )

    query_grad, key_grad, value_grad = lax.map(
        backward_one, (query_use, key_use, value_use, doc_ids, log_totals, mixed_grad)
    )
    query_grad = rotate_back(query_grad, query_cos, query_sin).reshape(row_count, query_cols)
    key_grad = rotate_back(key_grad, key_cos, key_sin).reshape(row_count, key_cols)
    qkv_grad = jnp.concatenate(
        [query_grad, key_grad, value_grad.reshape(row_count, key_cols)], axis=1
    ).astype(jnp.bfloat16)
    grad_qkv = weight_grad(first_in, qkv_grad, block_size)
    first_grad = sum_rows(project_back(qkv_grad, w_qkv))
    unit_share = row_share(first_unit)
    input_part = middle_grad + normalize_back(
        first_grad, unit_share, row_share(first_scale), norm_gains[0]
    )
    first_gain = jnp.sum(first_grad * unit_share, axis=0)
    gain_part = jnp.stack([first_gain, second_gain], axis=0)
    input_grad, gain_rows = (
        lax.all_gather(input_part.astype(jnp.bfloat16), "mp", axis=0, tiled=True).astype(
            jnp.float32
        ),
        lax.all_gather(gain_part, "mp", axis=0, tiled=True),
    )
    gain_terms = jnp.sum(gain_rows.reshape(mp_count, 2, model_width), axis=0)
    in_grads = jnp.concatenate([grad_qkv, grad_gateup], axis=1).reshape(-1, block_size, block_size)
    out_grads = jnp.concatenate([grad_attn_out, grad_down], axis=0).reshape(
        -1, block_size, block_size
    )
    all_grads = jnp.concatenate([in_grads, out_grads], axis=0).astype(jnp.bfloat16)
    reduced, gain_sums = (
        lax.psum_scatter(
            jnp.concatenate([all_grads[rank * own : (rank + 1) * own] for rank in ring], axis=0),
            "dp",
            scatter_dimension=0,
            tiled=True,
            axis_index_groups=[ring],
        ).astype(jnp.float32),
        lax.psum_scatter(gain_terms, "dp", scatter_dimension=1, tiled=True),
    )
    factor = float(row_count * dp_count) ** (-0.5)
    grads = reduced * factor
    gain_grads = gain_sums * factor
    new_left = 0.5 * left_stats + 0.5 * jnp.einsum("bij,bkj->bik", grads, grads, precision=highest)
    new_right = 0.5 * right_stats + 0.5 * jnp.einsum(
        "bji,bjk->bik", grads, grads, precision=highest
    )
    right_part = jnp.einsum("bij,bjk->bik", grads, right_roots, precision=highest)
    direction = jnp.einsum("bij,bjk->bik", left_roots, right_part, precision=highest)
    new_weights = weight_blocks - weight_rate * direction
    new_ema = average_decay * ema_blocks + (1.0 - average_decay) * new_weights
    share = model_width // dp_count
    gain_share = lax.dynamic_slice_in_dim(norm_gains, lax.axis_index("dp") * share, share, 1)
    new_gains = gain_share - gain_rate * gain_grads
    input_out = input_grad.reshape(sequences, length, model_width)
    return (
        block_out,
        input_out,
        grads,
        new_weights,
        new_ema,
        new_left,
        new_right,
        gain_grads,
        new_gains,
    )


def solution(mesh):
    in_specs = (
        P("dp", None, None),
        P("dp", None, None),
        P("dp", None),
        P("dp", None),
        P(),
        P(("dp", "mp"), None, None),
        P(("dp", "mp"), None, None),
        P(("dp", "mp"), None, None),
        P(("dp", "mp"), None, None),
        P(("dp", "mp"), None, None),
        P(("dp", "mp"), None, None),
    )
    out_specs = (
        P("dp", None, None),
        P("dp", None, None),
        P(("dp", "mp"), None, None),
        P(("dp", "mp"), None, None),
        P(("dp", "mp"), None, None),
        P(("dp", "mp"), None, None),
        P(("dp", "mp"), None, None),
        P(None, "dp"),
        P(None, "dp"),
    )
    return jax.shard_map(
        on_device, mesh=mesh, in_specs=in_specs, out_specs=out_specs, check_vma=False
    )
```

profile of v0, /device:TPU:0, one launch (start us, length us, event | category | flops | bytes accessed | tf_op | source)
XLA Modules:
  0.0 1200.5 jit_solution(14629774651332840294)
XLA Ops:
  12.0 14.3 %convert_bitcast_fusion.2 = (f32[1024,2048]{1,0:T(8,128)}, f32[128,8,16,128]{3,1,2,0:T(8,128)}, f32[1,1024,2048]{2,1,0:T(8,128)}) fusion(bf16[1,1024,2048]{2,1,0:T(8,128)(2,1)} %param.11), kind=kLoop, calls=%fused_computation.50 | loop fusion | flops 2097152 | bytes 29360128 | tf_op jit(solution)/shard_map/reshape | solution.py:238
  26.3 8.7 copy.178
  41.2 188.6 %all-gather.7.cloned.1.call-done = bf16[672,128,128]{2,1,0:T(8,128)(2,1)} async-done(((bf16[84,128,128]{2,1,0:T(8,128)(2,1)}), bf16[672,128,128]{2,1,0:T(8,128)(2,1)}) %all-gather.7.cloned.1.call-update) | async-done | bytes 22020112 | tf_op jit(solution)/shard_map/all_gather | solution.py:225
  253.6 7.7 slice.234
  271.6 9.0 fusion.76
  282.1 7.2 fusion.148
  289.2 8.0 fusion.7
  297.3 7.4 fusion.86
  304.8 7.6 fusion.149
  312.4 8.2 fusion.6
  320.7 9.0 fusion.83
  340.5 44.6 %reduce-scatter.9.cloned.1.call-done = bf16[256,2048]{1,0:T(8,128)(2,1)} async-done(((bf16[1024,2048]{1,0:T(8,128)(2,1)}), bf16[256,2048]{1,0:T(8,128)(2,1)}) %reduce-scatter.9.cloned.1.call-update) | async-done | bytes 1048592 | tf_op jit(solution)/shard_map/reduce_scatter | solution.py:182
  395.3 12.5 %slice_bitcast_fusion.3 = (bf16[16,128,22,128]{3,1,2,0:T(8,128)(2,1)S(1)}, bf16[16,22,128,128]{3,2,1,0:T(8,128)(2,1)}) fusion(bf16[16,27,128,128]{3,2,1,0:T(8,128)(2,1)} %bitcast.372), kind=kLoop, calls=%fused_computation.222 | loop fusion | bytes 34603008 | tf_op jit(solution)/shard_map/tcj,rcij->tri/dot_general | solution.py:83
  407.7 5.4 copy.118
  413.1 15.1 %copy.173 = bf16[16,22,128,128]{2,3,1,0:T(8,128)(2,1)} copy(bf16[16,22,128,128]{3,2,1,0:T(8,128)(2,1)} %get-tuple-element.102) | data formatting | bytes 23068672
  438.3 18.9 %convolution_bitcast_fusion = f32[1024,2816]{1,0:T(8,128)} fusion(bf16[2816,128,16]{1,0,2:T(8,128)(2,1)} %bitcast.384, bf16[1024,2048]{1,0:T(8,128)(2,1)} %all-gather.9.cloned.1.call-done), kind=kOutput, calls=%fused_computation.49 | convolution fusion | flops 11811160064 | bytes 27262976 | tf_op jit(solution)/shard_map/tri,rcij->tcj/dot_general | solution.py:75
  457.2 15.0 %fusion.30 = (bf16[1024,1408]{1,0:T(8,128)(2,1)}, bf16[1024,1408]{1,0:T(8,128)(2,1)}, bf16[1024,1408]{1,0:T(8,128)(2,1)}) fusion(f32[1024,2816]{1,0:T(8,128)} %convolution_bitcast_fusion, bf16[1408,16,128]{2,0,1:T(8,128)(2,1)S(1)} %bitcast.389, bf16[1024,16,128]{2,1,0:T(8,128)(2,1)} %bitcast.395), kind=kOutput, calls=%fused_computation.59 | convolution fusion | flops 5928648704 | bytes 30146560 | tf_op jit(solution)/shard_map/tcj,rcij->tri/dot_general | solution.py:83
  490.3 18.1 %bitcast_convert_fusion.1 = bf16[1024,2048]{1,0:T(8,128)(2,1)} fusion(bf16[2048,22,128]{2,0,1:T(8,128)(2,1)} %bitcast.383, bf16[1024,11,128]{2,0,1:T(8,128)(2,1)} %copy.117, bf16[1024,11,128]{2,0,1:T(8,128)(2,1)} %copy.116), kind=kOutput, calls=%fused_computation.34 | convolution fusion | flops 11816140800 | bytes 21495808 | tf_op jit(solution)/shard_map/tcj,rcij->tri/dot_general | solution.py:83
  508.5 8.4 copy.110
  521.9 11.0 bitcast_convert_fusion.2
  533.0 6.6 convert_bitcast_fusion.1
  539.6 13.7 %reduce-scatter.13.cloned.1.call-done = bf16[256,2048]{1,0:T(8,128)(2,1)} async-done(((bf16[1024,2048]{1,0:T(8,128)(2,1)}), bf16[256,2048]{1,0:T(8,128)(2,1)}) %reduce-scatter.13.cloned.1.call-update) | async-done | bytes 1048592 | tf_op jit(solution)/shard_map/reduce_scatter | solution.py:182
  555.3 45.5 %reduce-scatter.11.cloned.1.call-done = bf16[256,2048]{1,0:T(8,128)(2,1)} async-done(((bf16[1024,2048]{1,0:T(8,128)(2,1)}), bf16[256,2048]{1,0:T(8,128)(2,1)}) %reduce-scatter.11.cloned.1.call-update) | async-done | bytes 1048592 | tf_op jit(solution)/shard_map/reduce_scatter | solution.py:182
  611.2 29.3 %all-gather.13.cloned.1.call-done = bf16[1024,2048]{1,0:T(8,128)(2,1)} async-done(((bf16[256,2048]{1,0:T(8,128)(2,1)}), bf16[1024,2048]{1,0:T(8,128)(2,1)}) %all-gather.13.cloned.1.call-update) | async-done | bytes 4194320 | tf_op jit(solution)/shard_map/all_gather | solution.py:281
  640.6 5.2 bitcast_convert_fusion.5
  645.9 7.4 fusion.92
  653.3 13.0 %fusion.3 = (f32[8,512]{1,0:T(8,128)S(1)}, f32[1024,512,8]{1,0,2:T(8,128)}) fusion(f32[1,8,512,1024]{2,3,1,0:T(8,128)} %get-tuple-element.131, f32[8,512]{1,0:T(8,128)S(1)} %log_add_fusion.1, bf16[512,8,64]{0,2,1:T(8,128)(2,1)S(1)} %bitcast.394, f32[1024,640]{0,1:T(8,128)} %copy-done.15), kind=kOutput, calls=%fused_computation.9 | convolution fusion | flops 549449728 | bytes 34242560 | tf_op jit(solution)/shard_map/while/body/eval_jaxpr/qgjd,kgd->gjqk/dot_general | solution.py:158
  667.0 8.3 fusion
  675.3 7.9 fusion.18
  690.3 12.2 %fusion.17 = bf16[8,512,1024]{1,2,0:T(8,128)(2,1)S(1)} fusion(f32[1024,512,8]{1,0,2:T(8,128)} %get-tuple-element.135, f32[1,8,512,1024]{2,3,1,0:T(8,128)} %get-tuple-element.131, f32[8,512]{1,0:T(8,128)S(1)} %get-tuple-element.134, f32[8,512]{1,0:T(8,128)S(1)} %log_add_fusion.1), kind=kLoop, calls=%fused_computation.31 | loop fusion | flops 16777216 | bytes 41975808 | tf_op jit(solution)/shard_map/reshape.88
  724.0 35.0 %reduce-scatter.15.cloned.1.call-done = bf16[256,2048]{1,0:T(8,128)(2,1)} async-done(((bf16[1024,2048]{1,0:T(8,128)(2,1)}), bf16[256,2048]{1,0:T(8,128)(2,1)}) %reduce-scatter.15.cloned.1.call-update) | async-done | bytes 1048592 | tf_op jit(solution)/shard_map/reduce_scatter | solution.py:182
  761.7 5.2 all-gather
  772.1 16.0 %convert_bitcast_fusion = bf16[16,22,128,128]{2,3,0,1:T(8,128)(2,1)S(1)} fusion(bf16[1024,11,128]{2,0,1:T(8,128)(2,1)} %copy.117, bf16[1024,11,128]{2,0,1:T(8,128)(2,1)} %copy.116, bf16[1024,2048]{1,0:T(8,128)(2,1)} %all-gather.9.cloned.1.call-done), kind=kOutput, calls=%fused_computation.23 | convolution fusion | flops 11828461568 | bytes 21495808 | tf_op jit(solution)/shard_map/tri,tcj->rcij/dot_general | solution.py:92
  788.2 11.2 convert_bitcast_fusion.4
  803.1 8.1 pad_maximum_fusion
  811.3 18.9 %copy.132 = bf16[16,27,128,128]{3,2,1,0:T(8,128)(2,1)} copy(bf16[16,27,128,128]{2,3,0,1:T(8,128)(2,1)} %pad_maximum_fusion) | data formatting | bytes 28311552 | tf_op jit(solution)/shard_map/concatenate | solution.py:317
  836.6 6.6 pad_maximum_fusion.1
  843.2 10.7 copy.138
  879.3 6.1 copy.140
  885.4 6.1 copy.141
  897.5 6.7 bitcast_convert_fusion.4
  904.2 212.1 %reduce-scatter.17.cloned.1.call-done = bf16[84,128,128]{2,1,0:T(8,128)(2,1)} async-done(((bf16[672,128,128]{2,1,0:T(8,128)(2,1)}), bf16[84,128,128]{2,1,0:T(8,128)(2,1)}) %reduce-scatter.17.cloned.1.call-update) | async-done | bytes 2752528 | tf_op jit(solution)/shard_map/reduce_scatter | solution.py:323
  1121.5 11.9 fusion.154
  1133.5 16.3 %multiply_add_fusion = (f32[84,128,128]{1,2,0:T(8,128)}, f32[84,128,128]{1,2,0:T(8,128)}) fusion(f32[84,128,128]{1,2,0:T(8,128)S(1)} %bitcast.380, f32[84,128,128]{1,2,0:T(8,128)S(1)} %bitcast.378, f32[84,128,128]{1,2,0:T(8,128)S(1)} %fusion.154, f32[84,128,128]{2,1,0:T(8,128)} %param.20), kind=kOutput, calls=%fused_computation.69 | convolution fusion | flops 2119434240 | bytes 33030144 | tf_op jit(solution)/shard_map/bij,bjk->bik/dot_general | solution.py:340
  1149.8 6.1 copy.143
  1155.9 6.2 copy.144
  1162.1 17.2 %add_multiply_fusion.1 = f32[84,128,128]{2,1,0:T(8,128)} fusion(f32[84,128,128]{2,1,0:T(8,128)} %param.18, f32[84,128,128]{2,1,0:T(8,128)} %copy-done), kind=kOutput, calls=%fused_computation.68 | convolution fusion | flops 2116681728 | bytes 16515072 | tf_op jit(solution)/shard_map/bij,bkj->bik/dot_general | solution.py:335
  1179.3 12.6 %add_multiply_fusion = f32[84,128,128]{2,1,0:T(8,128)} fusion(f32[84,128,128]{2,1,0:T(8,128)} %param.19, f32[84,128,128]{2,1,0:T(8,128)S(1)} %bitcast.360), kind=kOutput, calls=%fused_computation.67 | convolution fusion | flops 2116681728 | bytes 16515072 | tf_op jit(solution)/shard_map/bji,bjk->bik/dot_general | solution.py:336
  (269 shorter events, 198.8 us)
Async XLA Ops:
  7.2 222.6 %all-gather.7.cloned.1.call-start = ((), (), s32[]{:S(2)}) async-start(), calls=%async_computation.6 | async-start | bytes 24772608 | tf_op jit(solution)/shard_map/all_gather | solution.py:225
  11.9 373.2 %reduce-scatter.9.cloned.1.call-start = ((), (), s32[]{:S(2)}) async-start(), calls=%async_computation.7 | async-start | bytes 5242880 | tf_op jit(solution)/shard_map/reduce_scatter | solution.py:182
  35.8 245.0 %copy-start.50 = (f32[32]{0:T(128)}, f32[32]{0:T(128)S(1)}, u32[]{:S(2)}) copy-start(f32[32]{0:T(128)S(1)} %negate_power_fusion) | copy-start | bytes 388
  39.0 232.6 %copy-start.47 = (f32[1024]{0:T(1024)}, f32[1024]{0:T(1024)S(1)}, u32[]{:S(2)}) copy-start(f32[1024]{0:T(1024)S(1)} %add_rsqrt_fusion) | copy-start | bytes 12292
  39.1 241.8 %copy-start.40 = (f32[1024]{0:T(1024)}, f32[1024]{0:T(1024)S(1)}, u32[]{:S(2)}) copy-start(f32[1024]{0:T(1024)S(1)} %fusion.134) | copy-start | bytes 12292
  39.6 241.8 %copy-start.28 = (f32[1024,32]{0,1:T(8,128)}, f32[1024,32]{0,1:T(8,128)S(1)}, u32[]{:S(2)}) copy-start(f32[1024,32]{0,1:T(8,128)S(1)} %get-tuple-element.120) | copy-start | bytes 393220
  39.6 241.8 %copy-start.30 = (f32[1024,32]{0,1:T(8,128)}, f32[1024,32]{0,1:T(8,128)S(1)}, u32[]{:S(2)}) copy-start(f32[1024,32]{0,1:T(8,128)S(1)} %get-tuple-element.121) | copy-start | bytes 393220
  41.1 230.5 %copy-start.38 = (f32[1,2048]{1,0:T(1,128)}, f32[1,2048]{1,0:T(1,128)S(1)}, u32[]{:S(2)}) copy-start(f32[1,2048]{1,0:T(1,128)S(1)} %get-tuple-element.119) | copy-start | bytes 24580
  229.8 20.0 %copy-start.3 = (bf16[672,128,128]{2,1,0:T(8,128)(2,1)S(1)}, bf16[672,128,128]{2,1,0:T(8,128)(2,1)}, u32[]{:S(2)}) copy-start(bf16[672,128,128]{2,1,0:T(8,128)(2,1)} %all-gather.7.cloned.1.call-done) | copy-start | bytes 66060292
  280.6 16.6 %copy-start.15 = (f32[1024,640]{0,1:T(8,128)}, f32[1024,640]{0,1:T(8,128)S(1)}, u32[]{:S(2)}) copy-start(f32[1024,640]{0,1:T(8,128)S(1)} %fusion.76) | copy-start | bytes 7864324
  281.4 23.3 %copy-start.22 = (bf16[1024,32]{0,1:T(8,128)(2,1)}, bf16[1024,32]{0,1:T(8,128)(2,1)S(1)}, u32[]{:S(2)}) copy-start(bf16[1024,32]{0,1:T(8,128)(2,1)S(1)} %get-tuple-element.116) | copy-start | bytes 196612
  281.4 23.3 %copy-start.24 = (bf16[1024,32]{0,1:T(8,128)(2,1)}, bf16[1024,32]{0,1:T(8,128)(2,1)S(1)}, u32[]{:S(2)}) copy-start(bf16[1024,32]{0,1:T(8,128)(2,1)S(1)} %get-tuple-element.117) | copy-start | bytes 196612
  281.8 23.0 %copy-start.4 = (bf16[1,1024,1,8,32]{1,4,3,2,0:T(8,128)(2,1)}, bf16[1,1024,1,8,32]{1,4,3,2,0:T(8,128)(2,1)S(1)}, u32[]{:S(2)}) copy-start(bf16[1,1024,1,8,32]{1,4,3,2,0:T(8,128)(2,1)S(1)} %get-tuple-element.109) | copy-start | bytes 1572868
  281.8 23.0 %copy-start.6 = (bf16[1,1024,1,8,32]{1,4,3,2,0:T(8,128)(2,1)}, bf16[1,1024,1,8,32]{1,4,3,2,0:T(8,128)(2,1)S(1)}, u32[]{:S(2)}) copy-start(bf16[1,1024,1,8,32]{1,4,3,2,0:T(8,128)(2,1)S(1)} %get-tuple-element.110) | copy-start | bytes 1572868
  304.8 31.1 %copy-start.17 = (bf16[64,8,512]{2,0,1:T(8,128)(2,1)}, bf16[64,8,512]{2,0,1:T(8,128)(2,1)S(1)}, u32[]{:S(2)}) copy-start(bf16[64,8,512]{2,0,1:T(8,128)(2,1)S(1)} %fusion.86) | copy-start | bytes 1572868
  312.4 17.3 %slice-start.8 = ((s8[22020096]{0:T(1024)(128)(4,1)}), s8[1048576]{0:T(1024)(128)(4,1)S(1)}, s32[]{:S(2)}) async-start(s8[22020096]{0:T(1024)(128)(4,1)} %bitcast.375), calls=%async_computation.25 | async-start | bytes 2097152
  312.4 17.3 %slice-start.9 = ((s8[22020096]{0:T(1024)(128)(4,1)}), s8[4194304]{0:T(1024)(128)(4,1)S(1)}, s32[]{:S(2)}) async-start(s8[22020096]{0:T(1024)(128)(4,1)} %bitcast.375), calls=%async_computation.26 | async-start | bytes 8388608
  320.6 9.0 slice-start.10
  320.7 9.5 slice-start.12
  320.7 10.7 slice-start.13
  331.4 9.1 copy-start.19
  340.5 48.3 %copy-start.52 = (s32[1,1024]{1,0:T(1,128)S(1)}, s32[1,1024]{1,0:T(1,128)}, u32[]{:S(2)}) copy-start(s32[1,1024]{1,0:T(1,128)} %param.13) | copy-start | bytes 12292
  340.5 97.8 %all-gather.9.cloned.1.call-start = ((), (), s32[]{:S(2)}) async-start(), calls=%async_computation.8 | async-start | bytes 5242880 | tf_op jit(solution)/shard_map/all_gather | solution.py:257
  388.7 164.6 %reduce-scatter.13.cloned.1.call-start = ((), (), s32[]{:S(2)}) async-start(), calls=%async_computation.11 | async-start | bytes 5242880 | tf_op jit(solution)/shard_map/reduce_scatter | solution.py:182
  438.3 18.9 %copy-start.11 = (bf16[11,16,128,128]{3,2,0,1:T(8,128)(2,1)S(1)}, bf16[11,16,128,128]{3,2,0,1:T(8,128)(2,1)}, u32[]{:S(2)}) copy-start(bf16[11,16,128,128]{3,2,0,1:T(8,128)(2,1)} %copy.112) | copy-start | bytes 17301508
  508.5 92.3 %reduce-scatter.11.cloned.1.call-start = ((), (), s32[]{:S(2)}) async-start(), calls=%async_computation.9 | async-start | bytes 5242880 | tf_op jit(solution)/shard_map/reduce_scatter | solution.py:182
  532.8 107.7 %all-gather.13.cloned.1.call-start = ((), (), s32[]{:S(2)}) async-start(), calls=%async_computation.12 | async-start | bytes 5242880 | tf_op jit(solution)/shard_map/all_gather | solution.py:281
  605.9 153.0 %reduce-scatter.15.cloned.1.call-start = ((), (), s32[]{:S(2)}) async-start(), calls=%async_computation.13 | async-start | bytes 5242880 | tf_op jit(solution)/shard_map/reduce_scatter | solution.py:182
  645.9 20.4 %slice-start = ((s8[16777216]{0:T(1024)(128)(4,1)}), s8[4194304]{0:T(1024)(128)(4,1)S(1)}, s32[]{:S(2)}) async-start(s8[16777216]{0:T(1024)(128)(4,1)} %bitcast.357), calls=%async_computation.17 | async-start | bytes 8388608
  645.9 20.4 %slice-start.1 = ((s8[16777216]{0:T(1024)(128)(4,1)}), s8[4194304]{0:T(1024)(128)(4,1)S(1)}, s32[]{:S(2)}) async-start(s8[16777216]{0:T(1024)(128)(4,1)} %bitcast.357), calls=%async_computation.18 | async-start | bytes 8388608
  653.3 13.0 %slice-start.2 = ((s8[16777216]{0:T(1024)(128)(4,1)}), s8[4194304]{0:T(1024)(128)(4,1)S(1)}, s32[]{:S(2)}) async-start(s8[16777216]{0:T(1024)(128)(4,1)} %bitcast.357), calls=%async_computation.19 | async-start | bytes 8388608
  653.3 13.7 %slice-start.3 = ((s8[16777216]{0:T(1024)(128)(4,1)}), s8[4194304]{0:T(1024)(128)(4,1)S(1)}, s32[]{:S(2)}) async-start(s8[16777216]{0:T(1024)(128)(4,1)} %bitcast.357), calls=%async_computation.20 | async-start | bytes 8388608
  714.3 177.2 %all-gather.11.cloned.1.call-start = ((), (), s32[]{:S(2)}) async-start(), calls=%async_computation.10 | async-start | bytes 5242880 | tf_op jit(solution)/shard_map/all_gather | solution.py:264
  715.1 176.4 %reduce-scatter.19.cloned.1.call-start = ((), (), s32[]{:S(2)}) async-start(), calls=%async_computation.16 | async-start | bytes 1179648
  722.0 46.5 %copy-start.10 = (f32[256,2048]{1,0:T(8,128)S(1)}, f32[256,2048]{1,0:T(8,128)}, u32[]{:S(2)}) copy-start(f32[256,2048]{1,0:T(8,128)} %get-tuple-element.92) | copy-start | bytes 6291460
  759.0 9.5 copy-start.14
  768.4 129.1 %all-gather.15.cloned.1.call-start = ((), (), s32[]{:S(2)}) async-start(), calls=%async_computation.14 | async-start | bytes 5242880 | tf_op jit(solution)/shard_map/all_gather | solution.py:311
  772.1 344.2 %reduce-scatter.17.cloned.1.call-start = ((), (), s32[]{:S(2)}) async-start(), calls=%async_computation.15 | async-start | bytes 24772608 | tf_op jit(solution)/shard_map/reduce_scatter | solution.py:323
  788.2 11.2 copy-start.13
  788.2 11.2 copy-start.27
  853.8 11.4 slice-start.6
  1116.3 17.2 %slice-start.15 = ((s8[5505024]{0:T(1024)(128)(4,1)}), s8[4194304]{0:T(1024)(128)(4,1)S(1)}, s32[]{:S(2)}) async-start(s8[5505024]{0:T(1024)(128)(4,1)} %bitcast.377), calls=%async_computation.32 | async-start | bytes 8388608
  1116.3 17.2 %slice-start.17 = ((s8[5505024]{0:T(1024)(128)(4,1)}), s8[4194304]{0:T(1024)(128)(4,1)S(1)}, s32[]{:S(2)}) async-start(s8[5505024]{0:T(1024)(128)(4,1)} %bitcast.379), calls=%async_computation.34 | async-start | bytes 8388608
  1121.5 12.0 slice-start.16
  1121.5 12.0 slice-start.18
  1155.9 23.3 %slice-start.4 = ((s8[5505024]{0:T(1024)(128)(4,1)}), s8[1310720]{0:T(1024)(128)(4,1)S(1)}, s32[]{:S(2)}) async-start(s8[5505024]{0:T(1024)(128)(4,1)} %bitcast.359), calls=%async_computation.21 | async-start | bytes 2621440
  1162.1 17.2 %slice-start.5 = ((s8[5505024]{0:T(1024)(128)(4,1)}), s8[4194304]{0:T(1024)(128)(4,1)S(1)}, s32[]{:S(2)}) async-start(s8[5505024]{0:T(1024)(128)(4,1)} %bitcast.359), calls=%async_computation.22 | async-start | bytes 8388608
  1179.2 12.6 %copy-start.12 = (bf16[1024,2048]{1,0:T(8,128)(2,1)S(1)}, bf16[1024,2048]{1,0:T(8,128)(2,1)}, u32[]{:S(2)}) copy-start(bf16[1024,2048]{1,0:T(8,128)(2,1)} %all-gather.11.cloned.1.call-done) | copy-start | bytes 12582916
  (35 other events, 169.8 us)
Sparse Core Ops, SparseCore 0:
  12.0 217.6 all-gather.6
  340.6 44.5 reduce-scatter.8
  388.8 34.4 all-gather.8
  508.6 44.6 reduce-scatter.12
  556.3 44.4 reduce-scatter.10
  606.1 34.4 all-gather.12
  714.4 44.4 reduce-scatter.14
  760.5 34.4 all-gather.10
  798.4 63.4 reduce-scatter.18
  864.0 33.4 all-gather.14
  900.0 216.2 reduce-scatter.16
where the time goes:
time: 1210 us; the launch traced here: 1200 us
  waiting for transfers between devices  574 us (47%)
  matrix products  249 us (21%)
  local copies, waits for them, and re-layouts  235 us (19%)
  other arithmetic  122 us (10%)
  between operations  15.1 us (1%)
    reduce_scatter x1, waiting for transfers between devices, on_device(): lax.psum_scatter(jnp.concatenate([all_grads[rank * own:(rank + 1) * own]...  212 us
    all_gather x1, waiting for transfers between devices, on_device(): lax.all_gather(weights_low, 'dp', axis=0, tiled=True, axis_index_groups=[...  189 us
    reduce_scatter x4, waiting for transfers between devices, sum_rows(): lax.psum_scatter(values.astype(jnp.bfloat16), 'mp', scatter_dimension=0,...  139 us
    unnamed x165, local copies, waits for them, and re-layouts  119 us
    dot_general x4, matrix products, project_back(): jnp.einsum('tcj,rcij->tri', shaped, weights, preferred_element_type=jnp.f...  43.4 us
    dot_general x4, matrix products, project(): jnp.einsum('tri,rcij->tcj', shaped, weights, preferred_element_type=jnp.f...  43.3 us
    dot_general x4, matrix products, weight_grad(): jnp.einsum('tri,tcj->rcij', left_shaped, right_shaped, preferred_element_...  33.7 us
    all_gather x1, waiting for transfers between devices, on_device(): lax.all_gather(middle_grad.astype(jnp.bfloat16), 'mp', axis=0, tiled=True)  29.3 us
  transfers between devices with their start and end apart: 11, of which 8 were waited for; matrix products, arithmetic and copies ran while one was open for 21% of the time, Pallas kernels for 0%

commit v1 on v0

--- a/solution.py
+++ b/solution.py
@@ -11,6 +11,13 @@
 weight_rate = 1.0
 gain_rate = 0.2
 average_decay = 0.9
+
+
+def exchange_gather(x, name, dim):
+    count = lax.axis_size(name)
+    tiles = jnp.stack([x for _ in range(count)])
+    tiles = lax.all_to_all(tiles, name, split_axis=0, concat_axis=0)
+    return jnp.concatenate(tiles, axis=dim)
 
 
 def doc_positions(doc_ids):
@@ -278,7 +285,7 @@
         second_grad, second_unit, second_scale, norm_gains[1]
     )
     second_gain = jnp.sum(second_grad * second_unit, axis=0)
-    attn_grad = lax.all_gather(middle_grad.astype(jnp.bfloat16), "mp", axis=0, tiled=True)
+    attn_grad = exchange_gather(middle_grad.astype(jnp.bfloat16), "mp", 0)
     grad_attn_out = weight_grad(mixed_use, attn_grad, block_size)
     mixed_grad = (
         project_back(attn_grad, w_attn_out)

time: 1210 us -> 1230 us (1.017)
  waiting for transfers between devices: 574 us -> 588 us
    all_to_all x0 -> x1, waiting for transfers between devices: none -> 43.6 us  [exchange_gather(): tiles = lax.all_to_all(tiles, name, split_axis=0, concat_axis=0)]
    all_gather x1 -> x0, waiting for transfers between devices: 29.3 us -> none  [on_device(): lax.all_gather(middle_grad.astype(jnp.bfloat16), 'mp', axis=0, tiled=True)]
    unnamed x165 -> x171, local copies, waits for them, and re-layouts: 119 us -> 121 us
where the time goes in v1:
time: 1230 us; the launch traced here: 1220 us
  waiting for transfers between devices  588 us (48%)
  matrix products  249 us (20%)
  local copies, waits for them, and re-layouts  237 us (19%)
  other arithmetic  122 us (10%)
  between operations  15.5 us (1%)
    reduce_scatter x1, waiting for transfers between devices, on_device(): lax.psum_scatter(jnp.concatenate([all_grads[rank * own:(rank + 1) * own]...  212 us
    all_gather x1, waiting for transfers between devices, on_device(): lax.all_gather(weights_low, 'dp', axis=0, tiled=True, axis_index_groups=[...  189 us
    reduce_scatter x4, waiting for transfers between devices, sum_rows(): lax.psum_scatter(values.astype(jnp.bfloat16), 'mp', scatter_dimension=0,...  139 us
    unnamed x171, local copies, waits for them, and re-layouts  121 us
    all_to_all x1, waiting for transfers between devices, exchange_gather(): tiles = lax.all_to_all(tiles, name, split_axis=0, concat_axis=0)  43.6 us
    dot_general x4, matrix products, project(): jnp.einsum('tri,rcij->tcj', shaped, weights, preferred_element_type=jnp.f...  43.3 us
    dot_general x4, matrix products, project_back(): jnp.einsum('tcj,rcij->tri', shaped, weights, preferred_element_type=jnp.f...  40.5 us
    dot_general x4, matrix products, weight_grad(): jnp.einsum('tri,tcj->rcij', left_shaped, right_shaped, preferred_element_...  35.9 us
  transfers between devices with their start and end apart: 11, of which 8 were waited for; matrix products, arithmetic and copies ran while one was open for 21% of the time, Pallas kernels for 0%

profile of v1, /device:TPU:0, one launch (start us, length us, event | category | flops | bytes accessed | tf_op | source)
XLA Modules:
  0.0 1221.6 jit_solution(11990858947721560008)
XLA Ops:
  12.0 14.3 %convert_bitcast_fusion.2 = (f32[1024,2048]{1,0:T(8,128)}, f32[128,8,16,128]{3,1,2,0:T(8,128)}, f32[1,1024,2048]{2,1,0:T(8,128)}) fusion(bf16[1,1024,2048]{2,1,0:T(8,128)(2,1)} %param.11), kind=kLoop, calls=%fused_computation.50 | loop fusion | flops 2097152 | bytes 29360128 | tf_op jit(solution)/shard_map/reshape | solution.py:245
  26.3 8.7 copy.176
  41.1 188.6 %all-gather.6.cloned.1.call-done = bf16[672,128,128]{2,1,0:T(8,128)(2,1)} async-done(((bf16[84,128,128]{2,1,0:T(8,128)(2,1)}), bf16[672,128,128]{2,1,0:T(8,128)(2,1)}) %all-gather.6.cloned.1.call-update) | async-done | bytes 22020112 | tf_op jit(solution)/shard_map/all_gather | solution.py:232
  253.6 7.7 slice.234
  271.6 9.0 fusion.75
  282.1 7.2 fusion.147
  289.2 8.0 fusion.7
  297.3 7.4 fusion.85
  304.8 7.6 fusion.148
  312.4 8.2 fusion.6
  320.7 9.0 fusion.82
  340.5 44.6 %reduce-scatter.9.cloned.1.call-done = bf16[256,2048]{1,0:T(8,128)(2,1)} async-done(((bf16[1024,2048]{1,0:T(8,128)(2,1)}), bf16[256,2048]{1,0:T(8,128)(2,1)}) %reduce-scatter.9.cloned.1.call-update) | async-done | bytes 1048592 | tf_op jit(solution)/shard_map/reduce_scatter | solution.py:189
  395.2 12.5 %slice_bitcast_fusion.3 = (bf16[16,128,22,128]{3,1,2,0:T(8,128)(2,1)S(1)}, bf16[16,22,128,128]{3,2,1,0:T(8,128)(2,1)}) fusion(bf16[16,27,128,128]{3,2,1,0:T(8,128)(2,1)} %bitcast.364), kind=kLoop, calls=%fused_computation.221 | loop fusion | bytes 34603008 | tf_op jit(solution)/shard_map/tcj,rcij->tri/dot_general | solution.py:90
  407.7 5.4 copy.117
  413.1 15.1 %copy.172 = bf16[16,22,128,128]{2,3,1,0:T(8,128)(2,1)} copy(bf16[16,22,128,128]{3,2,1,0:T(8,128)(2,1)} %get-tuple-element.102) | data formatting | bytes 23068672
  438.3 18.9 %convolution_bitcast_fusion = f32[1024,2816]{1,0:T(8,128)} fusion(bf16[2816,128,16]{1,0,2:T(8,128)(2,1)} %bitcast.376, bf16[1024,2048]{1,0:T(8,128)(2,1)} %all-gather.8.cloned.1.call-done), kind=kOutput, calls=%fused_computation.49 | convolution fusion | flops 11811160064 | bytes 27262976 | tf_op jit(solution)/shard_map/tri,rcij->tcj/dot_general | solution.py:82
  457.2 15.0 %fusion.30 = (bf16[1024,1408]{1,0:T(8,128)(2,1)}, bf16[1024,1408]{1,0:T(8,128)(2,1)}, bf16[1024,1408]{1,0:T(8,128)(2,1)}) fusion(f32[1024,2816]{1,0:T(8,128)} %convolution_bitcast_fusion, bf16[1408,16,128]{2,0,1:T(8,128)(2,1)S(1)} %bitcast.381, bf16[1024,16,128]{2,1,0:T(8,128)(2,1)} %bitcast.387), kind=kOutput, calls=%fused_computation.59 | convolution fusion | flops 5928648704 | bytes 30146560 | tf_op jit(solution)/shard_map/tcj,rcij->tri/dot_general | solution.py:90
  490.4 18.1 %bitcast_convert_fusion.1 = bf16[1024,2048]{1,0:T(8,128)(2,1)} fusion(bf16[2048,22,128]{2,0,1:T(8,128)(2,1)} %bitcast.375, bf16[1024,11,128]{2,0,1:T(8,128)(2,1)} %copy.116, bf16[1024,11,128]{2,0,1:T(8,128)(2,1)} %copy.115), kind=kOutput, calls=%fused_computation.34 | convolution fusion | flops 11816140800 | bytes 21495808 | tf_op jit(solution)/shard_map/tcj,rcij->tri/dot_general | solution.py:90
  508.6 8.4 copy.109
  521.8 11.0 bitcast_convert_fusion.2
  532.9 6.6 convert_bitcast_fusion.1
  539.5 13.8 %reduce-scatter.13.cloned.1.call-done = bf16[256,2048]{1,0:T(8,128)(2,1)} async-done(((bf16[1024,2048]{1,0:T(8,128)(2,1)}), bf16[256,2048]{1,0:T(8,128)(2,1)}) %reduce-scatter.13.cloned.1.call-update) | async-done | bytes 1048592 | tf_op jit(solution)/shard_map/reduce_scatter | solution.py:189
  555.3 45.5 %reduce-scatter.11.cloned.1.call-done = bf16[256,2048]{1,0:T(8,128)(2,1)} async-done(((bf16[1024,2048]{1,0:T(8,128)(2,1)}), bf16[256,2048]{1,0:T(8,128)(2,1)}) %reduce-scatter.11.cloned.1.call-update) | async-done | bytes 1048592 | tf_op jit(solution)/shard_map/reduce_scatter | solution.py:189
  617.6 43.6 %all-to-all-done = bf16[4,256,2048]{2,1,0:T(8,128)(2,1)} async-done(((bf16[4,256,2048]{2,1,0:T(8,128)(2,1)}), bf16[4,256,2048]{2,1,0:T(8,128)(2,1)}, u32[]{:S(2)}, u32[]{:S(2)}) %all-to-all-start) | async-done | bytes 4194336 | tf_op jit(solution)/shard_map/all_to_all | solution.py:19
  667.3 7.4 fusion.91
  674.6 13.0 %fusion.3 = (f32[8,512]{1,0:T(8,128)S(1)}, f32[1024,512,8]{1,0,2:T(8,128)}) fusion(f32[1,8,512,1024]{2,3,1,0:T(8,128)} %get-tuple-element.131, f32[8,512]{1,0:T(8,128)S(1)} %log_add_fusion.1, bf16[512,8,64]{0,2,1:T(8,128)(2,1)S(1)} %bitcast.386, f32[1024,640]{0,1:T(8,128)} %copy-done.17), kind=kOutput, calls=%fused_computation.9 | convolution fusion | flops 549449728 | bytes 34242560 | tf_op jit(solution)/shard_map/while/body/eval_jaxpr/qgjd,kgd->gjqk/dot_general | solution.py:165
  688.4 8.3 fusion
  696.6 7.9 fusion.18
  711.6 12.2 %fusion.17 = bf16[8,512,1024]{1,2,0:T(8,128)(2,1)S(1)} fusion(f32[1024,512,8]{1,0,2:T(8,128)} %get-tuple-element.135, f32[1,8,512,1024]{2,3,1,0:T(8,128)} %get-tuple-element.131, f32[8,512]{1,0:T(8,128)S(1)} %get-tuple-element.134, f32[8,512]{1,0:T(8,128)S(1)} %log_add_fusion.1), kind=kLoop, calls=%fused_computation.31 | loop fusion | flops 16777216 | bytes 41975808 | tf_op jit(solution)/shard_map/reshape.87
  730.6 5.0 bitcast_convert_fusion
  745.3 35.0 %reduce-scatter.15.cloned.1.call-done = bf16[256,2048]{1,0:T(8,128)(2,1)} async-done(((bf16[1024,2048]{1,0:T(8,128)(2,1)}), bf16[256,2048]{1,0:T(8,128)(2,1)}) %reduce-scatter.15.cloned.1.call-update) | async-done | bytes 1048592 | tf_op jit(solution)/shard_map/reduce_scatter | solution.py:189
  783.0 5.2 all-gather
  793.5 16.0 %convert_bitcast_fusion = bf16[16,22,128,128]{2,3,0,1:T(8,128)(2,1)S(1)} fusion(bf16[1024,11,128]{2,0,1:T(8,128)(2,1)} %copy.116, bf16[1024,11,128]{2,0,1:T(8,128)(2,1)} %copy.115, bf16[1024,2048]{1,0:T(8,128)(2,1)} %all-gather.8.cloned.1.call-done), kind=kOutput, calls=%fused_computation.23 | convolution fusion | flops 11828461568 | bytes 21495808 | tf_op jit(solution)/shard_map/tri,tcj->rcij/dot_general | solution.py:99
  809.5 11.2 convert_bitcast_fusion.4
  824.5 8.2 pad_maximum_fusion
  832.6 19.1 %copy.131 = bf16[16,27,128,128]{3,2,1,0:T(8,128)(2,1)} copy(bf16[16,27,128,128]{2,3,0,1:T(8,128)(2,1)} %pad_maximum_fusion) | data formatting | bytes 28311552 | tf_op jit(solution)/shard_map/concatenate | solution.py:324
  856.6 6.6 pad_maximum_fusion.1
  863.2 10.7 copy.137
  899.7 6.1 copy.139
  905.8 6.1 copy.140
  918.4 6.7 bitcast_convert_fusion.4
  925.1 211.9 %reduce-scatter.17.cloned.1.call-done = bf16[84,128,128]{2,1,0:T(8,128)(2,1)} async-done(((bf16[672,128,128]{2,1,0:T(8,128)(2,1)}), bf16[84,128,128]{2,1,0:T(8,128)(2,1)}) %reduce-scatter.17.cloned.1.call-update) | async-done | bytes 2752528 | tf_op jit(solution)/shard_map/reduce_scatter | solution.py:330
  1142.3 11.9 fusion.153
  1154.3 16.3 %multiply_add_fusion = (f32[84,128,128]{1,2,0:T(8,128)}, f32[84,128,128]{1,2,0:T(8,128)}) fusion(f32[84,128,128]{1,2,0:T(8,128)S(1)} %bitcast.372, f32[84,128,128]{1,2,0:T(8,128)S(1)} %bitcast.370, f32[84,128,128]{1,2,0:T(8,128)S(1)} %fusion.153, f32[84,128,128]{2,1,0:T(8,128)} %param.20), kind=kOutput, calls=%fused_computation.69 | convolution fusion | flops 2119434240 | bytes 33030144 | tf_op jit(solution)/shard_map/bij,bjk->bik/dot_general | solution.py:347
  1170.6 6.1 copy.142
  1176.7 6.2 copy.143
  1182.8 17.2 %add_multiply_fusion.1 = f32[84,128,128]{2,1,0:T(8,128)} fusion(f32[84,128,128]{2,1,0:T(8,128)} %param.18, f32[84,128,128]{2,1,0:T(8,128)} %copy-done), kind=kOutput, calls=%fused_computation.68 | convolution fusion | flops 2116681728 | bytes 16515072 | tf_op jit(solution)/shard_map/bij,bkj->bik/dot_general | solution.py:342
  1200.0 12.6 %add_multiply_fusion = f32[84,128,128]{2,1,0:T(8,128)} fusion(f32[84,128,128]{2,1,0:T(8,128)} %param.19, f32[84,128,128]{2,1,0:T(8,128)S(1)} %bitcast.352), kind=kOutput, calls=%fused_computation.67 | convolution fusion | flops 2116681728 | bytes 16515072 | tf_op jit(solution)/shard_map/bji,bjk->bik/dot_general | solution.py:343
  (275 shorter events, 205.4 us)
Async XLA Ops:
  7.2 222.6 %all-gather.6.cloned.1.call-start = ((), (), s32[]{:S(2)}) async-start(), calls=%async_computation.7 | async-start | bytes 24772608 | tf_op jit(solution)/shard_map/all_gather | solution.py:232
  11.9 373.2 %reduce-scatter.9.cloned.1.call-start = ((), (), s32[]{:S(2)}) async-start(), calls=%async_computation.8 | async-start | bytes 5242880 | tf_op jit(solution)/shard_map/reduce_scatter | solution.py:189
  35.8 245.0 %copy-start.53 = (f32[32]{0:T(128)}, f32[32]{0:T(128)S(1)}, u32[]{:S(2)}) copy-start(f32[32]{0:T(128)S(1)} %negate_power_fusion) | copy-start | bytes 388
  39.0 232.6 %copy-start.50 = (f32[1024]{0:T(1024)}, f32[1024]{0:T(1024)S(1)}, u32[]{:S(2)}) copy-start(f32[1024]{0:T(1024)S(1)} %add_rsqrt_fusion) | copy-start | bytes 12292
  39.1 241.8 %copy-start.43 = (f32[1024]{0:T(1024)}, f32[1024]{0:T(1024)S(1)}, u32[]{:S(2)}) copy-start(f32[1024]{0:T(1024)S(1)} %fusion.133) | copy-start | bytes 12292
  39.6 241.8 %copy-start.31 = (f32[1024,32]{0,1:T(8,128)}, f32[1024,32]{0,1:T(8,128)S(1)}, u32[]{:S(2)}) copy-start(f32[1024,32]{0,1:T(8,128)S(1)} %get-tuple-element.120) | copy-start | bytes 393220
  39.6 241.8 %copy-start.33 = (f32[1024,32]{0,1:T(8,128)}, f32[1024,32]{0,1:T(8,128)S(1)}, u32[]{:S(2)}) copy-start(f32[1024,32]{0,1:T(8,128)S(1)} %get-tuple-element.121) | copy-start | bytes 393220
  41.1 230.5 %copy-start.41 = (f32[1,2048]{1,0:T(1,128)}, f32[1,2048]{1,0:T(1,128)S(1)}, u32[]{:S(2)}) copy-start(f32[1,2048]{1,0:T(1,128)S(1)} %get-tuple-element.119) | copy-start | bytes 24580
  229.8 20.0 %copy-start.3 = (bf16[672,128,128]{2,1,0:T(8,128)(2,1)S(1)}, bf16[672,128,128]{2,1,0:T(8,128)(2,1)}, u32[]{:S(2)}) copy-start(bf16[672,128,128]{2,1,0:T(8,128)(2,1)} %all-gather.6.cloned.1.call-done) | copy-start | bytes 66060292
  280.6 16.6 %copy-start.17 = (f32[1024,640]{0,1:T(8,128)}, f32[1024,640]{0,1:T(8,128)S(1)}, u32[]{:S(2)}) copy-start(f32[1024,640]{0,1:T(8,128)S(1)} %fusion.75) | copy-start | bytes 7864324
  281.4 23.3 %copy-start.25 = (bf16[1024,32]{0,1:T(8,128)(2,1)}, bf16[1024,32]{0,1:T(8,128)(2,1)S(1)}, u32[]{:S(2)}) copy-start(bf16[1024,32]{0,1:T(8,128)(2,1)S(1)} %get-tuple-element.116) | copy-start | bytes 196612
  281.4 23.3 %copy-start.27 = (bf16[1024,32]{0,1:T(8,128)(2,1)}, bf16[1024,32]{0,1:T(8,128)(2,1)S(1)}, u32[]{:S(2)}) copy-start(bf16[1024,32]{0,1:T(8,128)(2,1)S(1)} %get-tuple-element.117) | copy-start | bytes 196612
  281.8 23.0 %copy-start.5 = (bf16[1,1024,1,8,32]{1,4,3,2,0:T(8,128)(2,1)}, bf16[1,1024,1,8,32]{1,4,3,2,0:T(8,128)(2,1)S(1)}, u32[]{:S(2)}) copy-start(bf16[1,1024,1,8,32]{1,4,3,2,0:T(8,128)(2,1)S(1)} %get-tuple-element.109) | copy-start | bytes 1572868
  281.8 23.0 %copy-start.7 = (bf16[1,1024,1,8,32]{1,4,3,2,0:T(8,128)(2,1)}, bf16[1,1024,1,8,32]{1,4,3,2,0:T(8,128)(2,1)S(1)}, u32[]{:S(2)}) copy-start(bf16[1,1024,1,8,32]{1,4,3,2,0:T(8,128)(2,1)S(1)} %get-tuple-element.110) | copy-start | bytes 1572868
  304.8 31.1 %copy-start.20 = (bf16[64,8,512]{2,0,1:T(8,128)(2,1)}, bf16[64,8,512]{2,0,1:T(8,128)(2,1)S(1)}, u32[]{:S(2)}) copy-start(bf16[64,8,512]{2,0,1:T(8,128)(2,1)S(1)} %fusion.85) | copy-start | bytes 1572868
  312.4 17.3 %slice-start.8 = ((s8[22020096]{0:T(1024)(128)(4,1)}), s8[1048576]{0:T(1024)(128)(4,1)S(1)}, s32[]{:S(2)}) async-start(s8[22020096]{0:T(1024)(128)(4,1)} %bitcast.367), calls=%async_computation.25 | async-start | bytes 2097152
  312.4 17.3 %slice-start.9 = ((s8[22020096]{0:T(1024)(128)(4,1)}), s8[4194304]{0:T(1024)(128)(4,1)S(1)}, s32[]{:S(2)}) async-start(s8[22020096]{0:T(1024)(128)(4,1)} %bitcast.367), calls=%async_computation.26 | async-start | bytes 8388608
  320.7 10.7 slice-start.13
  340.5 48.2 %copy-start.55 = (s32[1,1024]{1,0:T(1,128)S(1)}, s32[1,1024]{1,0:T(1,128)}, u32[]{:S(2)}) copy-start(s32[1,1024]{1,0:T(1,128)} %param.13) | copy-start | bytes 12292
  340.5 97.8 %all-gather.8.cloned.1.call-start = ((), (), s32[]{:S(2)}) async-start(), calls=%async_computation.9 | async-start | bytes 5242880 | tf_op jit(solution)/shard_map/all_gather | solution.py:264
  388.6 164.6 %reduce-scatter.13.cloned.1.call-start = ((), (), s32[]{:S(2)}) async-start(), calls=%async_computation.12 | async-start | bytes 5242880 | tf_op jit(solution)/shard_map/reduce_scatter | solution.py:189
  438.3 18.9 %copy-start.12 = (bf16[11,16,128,128]{3,2,0,1:T(8,128)(2,1)S(1)}, bf16[11,16,128,128]{3,2,0,1:T(8,128)(2,1)}, u32[]{:S(2)}) copy-start(bf16[11,16,128,128]{3,2,0,1:T(8,128)(2,1)} %copy.111) | copy-start | bytes 17301508
  508.5 92.2 %reduce-scatter.11.cloned.1.call-start = ((), (), s32[]{:S(2)}) async-start(), calls=%async_computation.10 | async-start | bytes 5242880 | tf_op jit(solution)/shard_map/reduce_scatter | solution.py:189
  608.0 53.1 %all-to-all-start = ((bf16[4,256,2048]{2,1,0:T(8,128)(2,1)}), bf16[4,256,2048]{2,1,0:T(8,128)(2,1)}, u32[]{:S(2)}, u32[]{:S(2)}) async-start(bf16[4,256,2048]{2,1,0:T(8,128)(2,1)} %stack.16), calls=%async_computation.3 | async-start | bytes 8388608 | tf_op jit(solution)/shard_map/all_to_all | solution.py:19
  613.0 167.3 %reduce-scatter.15.cloned.1.call-start = ((), (), s32[]{:S(2)}) async-start(), calls=%async_computation.13 | async-start | bytes 5242880 | tf_op jit(solution)/shard_map/reduce_scatter | solution.py:189
  617.5 47.2 %copy-start.19 = (bf16[4,16,128,128]{3,2,0,1:T(8,128)(2,1)S(1)}, bf16[4,16,128,128]{3,2,0,1:T(8,128)(2,1)}, u32[]{:S(2)}) copy-start(bf16[4,16,128,128]{3,2,0,1:T(8,128)(2,1)} %copy.118) | copy-start | bytes 6291460
  667.2 20.4 %slice-start = ((s8[16777216]{0:T(1024)(128)(4,1)}), s8[4194304]{0:T(1024)(128)(4,1)S(1)}, s32[]{:S(2)}) async-start(s8[16777216]{0:T(1024)(128)(4,1)} %bitcast.349), calls=%async_computation.17 | async-start | bytes 8388608
  667.2 20.4 %slice-start.1 = ((s8[16777216]{0:T(1024)(128)(4,1)}), s8[4194304]{0:T(1024)(128)(4,1)S(1)}, s32[]{:S(2)}) async-start(s8[16777216]{0:T(1024)(128)(4,1)} %bitcast.349), calls=%async_computation.18 | async-start | bytes 8388608
  674.6 13.0 %slice-start.2 = ((s8[16777216]{0:T(1024)(128)(4,1)}), s8[4194304]{0:T(1024)(128)(4,1)S(1)}, s32[]{:S(2)}) async-start(s8[16777216]{0:T(1024)(128)(4,1)} %bitcast.349), calls=%async_computation.19 | async-start | bytes 8388608
  674.6 13.7 %slice-start.3 = ((s8[16777216]{0:T(1024)(128)(4,1)}), s8[4194304]{0:T(1024)(128)(4,1)S(1)}, s32[]{:S(2)}) async-start(s8[16777216]{0:T(1024)(128)(4,1)} %bitcast.349), calls=%async_computation.20 | async-start | bytes 8388608
  735.6 176.3 %all-gather.10.cloned.1.call-start = ((), (), s32[]{:S(2)}) async-start(), calls=%async_computation.11 | async-start | bytes 5242880 | tf_op jit(solution)/shard_map/all_gather | solution.py:271
  736.4 175.6 %reduce-scatter.19.cloned.1.call-start = ((), (), s32[]{:S(2)}) async-start(), calls=%async_computation.16 | async-start | bytes 1179648
  743.3 46.5 %copy-start.11 = (f32[256,2048]{1,0:T(8,128)S(1)}, f32[256,2048]{1,0:T(8,128)}, u32[]{:S(2)}) copy-start(f32[256,2048]{1,0:T(8,128)} %get-tuple-element.92) | copy-start | bytes 6291460
  780.3 9.5 copy-start.16
  789.7 128.7 %all-gather.12.cloned.1.call-start = ((), (), s32[]{:S(2)}) async-start(), calls=%async_computation.14 | async-start | bytes 5242880 | tf_op jit(solution)/shard_map/all_gather | solution.py:318
  793.4 343.6 %reduce-scatter.17.cloned.1.call-start = ((), (), s32[]{:S(2)}) async-start(), calls=%async_computation.15 | async-start | bytes 24772608 | tf_op jit(solution)/shard_map/reduce_scatter | solution.py:330
  809.5 11.2 copy-start.15
  809.5 11.2 copy-start.30
  832.6 19.1 %copy-start.35 = (bf16[512,4,128]{2,0,1:T(8,128)(2,1)S(1)}, bf16[512,4,128]{2,0,1:T(8,128)(2,1)}, u32[]{:S(2)}) copy-start(bf16[512,4,128]{2,0,1:T(8,128)(2,1)} %copy.133) | copy-start | bytes 1572868
  832.6 19.1 %copy-start.36 = (bf16[512,4,128]{2,0,1:T(8,128)(2,1)S(1)}, bf16[512,4,128]{2,0,1:T(8,128)(2,1)}, u32[]{:S(2)}) copy-start(bf16[512,4,128]{2,0,1:T(8,128)(2,1)} %copy.132) | copy-start | bytes 1572868
  873.9 11.4 slice-start.6
  1137.0 17.2 %slice-start.15 = ((s8[5505024]{0:T(1024)(128)(4,1)}), s8[4194304]{0:T(1024)(128)(4,1)S(1)}, s32[]{:S(2)}) async-start(s8[5505024]{0:T(1024)(128)(4,1)} %bitcast.369), calls=%async_computation.32 | async-start | bytes 8388608
  1137.0 17.2 %slice-start.17 = ((s8[5505024]{0:T(1024)(128)(4,1)}), s8[4194304]{0:T(1024)(128)(4,1)S(1)}, s32[]{:S(2)}) async-start(s8[5505024]{0:T(1024)(128)(4,1)} %bitcast.371), calls=%async_computation.34 | async-start | bytes 8388608
  1142.3 12.0 slice-start.16
  1142.3 12.0 slice-start.18
  1176.6 23.3 %slice-start.4 = ((s8[5505024]{0:T(1024)(128)(4,1)}), s8[1310720]{0:T(1024)(128)(4,1)S(1)}, s32[]{:S(2)}) async-start(s8[5505024]{0:T(1024)(128)(4,1)} %bitcast.351), calls=%async_computation.21 | async-start | bytes 2621440
  1182.8 17.2 %slice-start.5 = ((s8[5505024]{0:T(1024)(128)(4,1)}), s8[4194304]{0:T(1024)(128)(4,1)S(1)}, s32[]{:S(2)}) async-start(s8[5505024]{0:T(1024)(128)(4,1)} %bitcast.351), calls=%async_computation.22 | async-start | bytes 8388608
  1200.0 12.6 %copy-start.13 = (bf16[1024,2048]{1,0:T(8,128)(2,1)S(1)}, bf16[1024,2048]{1,0:T(8,128)(2,1)}, u32[]{:S(2)}) copy-start(bf16[1024,2048]{1,0:T(8,128)(2,1)} %all-gather.10.cloned.1.call-done) | copy-start | bytes 12582916
  (38 other events, 196.2 us)
Sparse Core Ops, SparseCore 0:
  12.0 217.6 all-gather.5
  340.6 44.4 reduce-scatter.8
  388.8 34.4 all-gather.7
  508.6 44.5 reduce-scatter.12
  556.2 44.4 reduce-scatter.10
  735.7 44.4 reduce-scatter.14
  781.8 34.4 all-gather.9
  819.8 63.4 reduce-scatter.18
  884.9 33.4 all-gather.11
  920.8 216.2 reduce-scatter.16
